TPU v7x, 32 devices: a whole 2x2x4 slice. The times are simulated.
32 devices in a mesh: layer: 16 (over z, y, core), dp: 2 (over x).
Axes of the slice: x: 2, y: 2, z: 4, core: 2. Of those that a mesh axis runs over, the one named last changes fastest.
Arguments:
- c_guess: float32 [16, 256, 512], P('layer', 'dp'), may hold values from -6 to 6
- adj_guess: float32 [16, 256, 512], P('layer', 'dp'), may hold values from -6 to 6
- norm_gain: float32 [32, 512], P('layer'), may hold values from 0.5 to 1.5
- w_up: bfloat16 [32, 512, 2048], P('layer'), may hold values from -0.25 to 0.25
- w_down: bfloat16 [32, 2048, 512], P('layer'), may hold values from -0.125 to 0.125
- coarse_rate: float32 [16, 512], P('layer'), may hold values from 0.5 to 1
Outputs:
- c_points: float32 [16, 256, 512], P('layer', 'dp')
- adj_points: float32 [16, 256, 512], P('layer', 'dp')
- grad_up: float32 [32, 512, 2048], P('layer', 'dp')
- grad_down: float32 [32, 2048, 512], P('layer', 'dp')
All inputs are finite; a program needn't handle non-finite values.
Results may differ from a plain program's by a relative error of at most 0.018.
Values may be sent and summed in bfloat16 or wider, within the bound.
A program may use at most 64 MiB of HBM per device.

v0:
```python
import jax
import jax.numpy as jnp
from jax import lax
from jax.sharding import PartitionSpec as P

eps = 1e-06
step_length = 0.5


def carried_in(x, axis, combine, identity, reverse):
    size, here = (lax.axis_size(axis), lax.axis_index(axis))
    everything = jax.tree.map(lambda part: lax.all_gather(part, axis), x)
    start = jax.tree.map(
        lambda part, zero: jnp.broadcast_to(jnp.asarray(zero, part.dtype), part.shape), x, identity
    )

    def step(k, before):
        at = size - 1 - k if reverse else k
        reached = at > here if reverse else at < here
        new = combine(before, jax.tree.map(lambda part: part[at], everything))
        return jax.tree.map(lambda a, b: jnp.where(reached, a, b), new, before)

    return lax.fori_loop(0, size, step, start)


def normalize(state):
    inverse_rms = lax.rsqrt(jnp.mean(state * state, axis=-1, keepdims=True) + eps)
    return (state * inverse_rms, inverse_rms)


def layer_forward(state, gain_row, up_matrix, down_matrix):
    unit_state, inverse_rms = normalize(state)
    normed = (unit_state * gain_row).astype(jnp.bfloat16)
    preact = jnp.dot(normed, up_matrix, preferred_element_type=jnp.float32)
    hidden = jax.nn.silu(preact).astype(jnp.bfloat16)
    return state + step_length * jnp.dot(hidden, down_matrix, preferred_element_type=jnp.float32)


def layer_backward(state, cotangent, gain_row, up_matrix, down_matrix):
    unit_state, inverse_rms = normalize(state)
    normed = (unit_state * gain_row).astype(jnp.bfloat16)
    preact = jnp.dot(normed, up_matrix, preferred_element_type=jnp.float32)
    hidden = jax.nn.silu(preact).astype(jnp.bfloat16)
    sigmoid_pre = jax.nn.sigmoid(preact)
    out_grad = (step_length * cotangent).astype(jnp.bfloat16)
    hidden_grad = jnp.dot(out_grad, down_matrix.T, preferred_element_type=jnp.float32)
    pre_grad = (hidden_grad * sigmoid_pre * (1.0 + preact * (1.0 - sigmoid_pre))).astype(
        jnp.bfloat16
    )
    normed_grad = jnp.dot(pre_grad, up_matrix.T, preferred_element_type=jnp.float32)
    unit_grad = normed_grad * gain_row
    inner = jnp.mean(unit_grad * unit_state, axis=-1, keepdims=True)
    new_cotangent = cotangent + inverse_rms * (unit_grad - unit_state * inner)
    return (new_cotangent, normed, pre_grad, hidden, out_grad)


def block_forward(state, gains, ups, downs):
    for depth_index in range(gains.shape[0]):
        state = layer_forward(state, gains[depth_index], ups[depth_index], downs[depth_index])
    return state


def block_inputs(state, gains, ups, downs):
    inputs = [state]
    state = layer_forward(state, gains[0], ups[0], downs[0])
    inputs.append(state)
    return inputs


def block_backward(inputs, cotangent, gains, ups, downs):
    normed_list, pre_list, hidden_list, out_list = ([], [], [], [])
    for depth_index in reversed(range(gains.shape[0])):
        cotangent, normed, pre_grad, hidden, out_grad = layer_backward(
            inputs[depth_index], cotangent, gains[depth_index], ups[depth_index], downs[depth_index]
        )
        normed_list.insert(0, normed)
        pre_list.insert(0, pre_grad)
        hidden_list.insert(0, hidden)
        out_list.insert(0, out_grad)
    factors = (
        jnp.stack(normed_list),
        jnp.stack(pre_list),
        jnp.stack(hidden_list),
        jnp.stack(out_list),
    )
    return (cotangent, factors)


def compose(earlier, later):
    return (earlier[0] * later[0], later[0] * earlier[1] + later[1])


def shards(c_guess, adj_guess, norm_gain, w_up, w_down, coarse_rate):
    position = lax.axis_index("layer")
    devices = lax.axis_size("layer")
    leading = position == 0
    trailing = position == devices - 1
    start_state = c_guess[0]
    decay_rate = coarse_rate[0]
    identity_map = (jnp.ones_like(decay_rate), jnp.zeros_like(start_state))
    block_end = block_forward(start_state, norm_gain, w_up, w_down)
    forward_rate = jnp.where(leading, jnp.zeros_like(decay_rate), decay_rate)
    forward_shift = block_end - forward_rate * start_state
    _, carried = carried_in((forward_rate, forward_shift), "layer", compose, identity_map, False)
    point = jnp.where(leading, start_state, carried)
    inputs = block_inputs(point, norm_gain, w_up, w_down)
    adjoint_guess = adj_guess[0]
    begin, _ = block_backward(inputs, adjoint_guess, norm_gain, w_up, w_down)
    backward_rate = jnp.where(trailing, jnp.zeros_like(decay_rate), decay_rate)
    backward_shift = begin - backward_rate * adjoint_guess
    _, carried_back = carried_in(
        (backward_rate, backward_shift), "layer", compose, identity_map, True
    )
    adjoint = jnp.where(trailing, adjoint_guess, carried_back)
    _, factors = block_backward(inputs, adjoint, norm_gain, w_up, w_down)
    normed_all, pre_all, hidden_all, out_all = factors
    group = lax.axis_size("dp")
    member = lax.axis_index("dp")
    width_share = w_up.shape[1] // group
    hidden_share = w_up.shape[2] // group
    piece_normed = lax.all_gather(normed_all, "dp", axis=1, tiled=True)
    piece_pre = lax.all_gather(pre_all, "dp", axis=1, tiled=True)
    piece_hidden = lax.all_gather(hidden_all, "dp", axis=1, tiled=True)
    piece_out = lax.all_gather(out_all, "dp", axis=1, tiled=True)
    normed_cols = lax.dynamic_slice_in_dim(piece_normed, member * width_share, width_share, 2)
    hidden_cols = lax.dynamic_slice_in_dim(piece_hidden, member * hidden_share, hidden_share, 2)
    up_part = jnp.einsum("ltd,ltf->ldf", normed_cols, piece_pre, preferred_element_type=jnp.float32)
    down_part = jnp.einsum(
        "ltf,ltd->lfd", hidden_cols, piece_out, preferred_element_type=jnp.float32
    )
    return (point[None], adjoint[None], up_part, down_part)


def solution(mesh):
    return jax.shard_map(
        shards,
        mesh=mesh,
        in_specs=(
            P("layer", "dp", None),
            P("layer", "dp", None),
            P("layer", None),
            P("layer", None, None),
            P("layer", None, None),
            P("layer", None),
        ),
        out_specs=(
            P("layer", "dp", None),
            P("layer", "dp", None),
            P("layer", "dp", None),
            P("layer", "dp", None),
        ),
        check_vma=False,
    )
```

profile of v0, /device:TPU:0, one launch (start us, length us, event | category | flops | bytes accessed | tf_op | source)
XLA Modules:
  0.0 239.0 jit_solution(10892800529612794329)
XLA Ops:
  9.1 3.2 %multiply_reduce_fusion.5 = (f32[128]{0:T(128)S(1)}, f32[128,512]{1,0:T(8,128)S(1)}) fusion(bf16[2,2048,512]{2,1,0:T(8,128)(2,1)} %param.14, bf16[2,512,2048]{2,1,0:T(8,128)(2,1)} %param.13, f32[1,128,512]{2,1,0:T(8,128)} %param.10, f32[512]{0:T(512)S(1)} %bitcast.178, f32[128]{0:T(128)S(1)} %add_rsqrt_fusion.3), kind=kOutput, calls=%fused_computation.108 | convolution fusion | flops 538640256 | bytes 4983808 | tf_op jit(solution)/shard_map/dot_general | solution.py:36
  12.3 3.7 %fusion.76 = f32[128,512]{1,0:T(8,128)} fusion(f32[128,512]{1,0:T(8,128)S(1)} %get-tuple-element.301, bf16[2,2048,512]{2,1,0:T(8,128)(2,1)} %param.14, bf16[2,512,2048]{2,1,0:T(8,128)(2,1)} %param.13, f32[1,128,512]{2,1,0:T(8,128)S(1)} %copy-done.3, f32[512]{0:T(512)S(1)} %bitcast.184, f32[512]{0:T(512)S(1)} %bitcast.173, f32[128]{0:T(128)S(1)} %add_rsqrt_fusion.2), kind=kOutput, calls=%fused_computation.66 | convolution fusion | flops 538640384 | bytes 5247488 | tf_op jit(solution)/shard_map/dot_general | solution.py:36
  16.1 23.3 %all-gather.2 = f32[16,1,512]{2,1,0:T(1,128)S(1)} all-gather(f32[1,1,512]{2,1,0:T(1,128)S(1)} %bitcast.185), channel_id=1, replica_groups=mesh['layer'=16,'dp'=2] {'layer'}, dimensions={0}, use_global_device_ids=true | all-gather | bytes 34816 | tf_op jit(solution)/shard_map/all_gather | solution.py:12
  39.4 29.9 %all-gather.13.cloned.1.call-done = f32[2048,512]{1,0:T(8,128)} async-done(((f32[128,512]{1,0:T(8,128)}), f32[2048,512]{1,0:T(8,128)}) %all-gather.13.cloned.1.call-update) | async-done | bytes 4194320 | tf_op jit(solution)/shard_map/all_gather | solution.py:12
  69.3 19.1 %while.30 = (s32[]{:T(128)}, f32[128,512]{1,0:T(8,128)S(1)}, s32[]{:T(128)}, f32[16,512]{1,0:T(8,128)S(1)}, f32[16,128,512]{2,1,0:T(8,128)}, /*index=5*/s32[]{:T(128)}, s32[]{:T(128)}) while((s32[]{:T(128)}, f32[128,512]{1,0:T(8,128)S(1)}, s32[]{:T(128)}, f32[16,512]{1,0:T(8,128)S(1)}, f32[16,128,512]{2,1,0:T(8,128)}, ...), condition=%wide.region_3.4_spmd.clone, body=%wide.region_2.3_spmd.clone.sunk | while | flops 262148 | bytes 792689 | solution.py:23
  70.5 1.2 fusion.150
  71.7 1.2 fusion.150
  72.9 1.2 fusion.150
  74.1 1.2 fusion.150
  75.3 1.2 fusion.150
  76.5 1.2 fusion.150
  77.7 1.2 fusion.150
  78.9 1.2 fusion.150
  80.1 1.2 fusion.150
  81.3 1.2 fusion.150
  82.5 1.2 fusion.150
  83.7 1.2 fusion.150
  84.9 1.2 fusion.150
  86.1 1.2 fusion.150
  87.3 1.2 fusion.150
  88.6 2.2 fusion.31
  92.0 1.5 copy-done.1
  94.1 4.5 %multiply_reduce_fusion.2 = (f32[128]{0:T(128)S(1)}, f32[128,512]{1,0:T(8,128)}) fusion(f32[128,512]{1,0:T(8,128)S(1)} %get-tuple-element.303, f32[128]{0:T(128)S(1)} %add_rsqrt_fusion, f32[512]{0:T(512)S(1)} %bitcast.175, bf16[2,512,2048]{2,1,0:T(8,128)(2,1)} %param.13, bf16[2,2048,512]{2,1,0:T(8,128)(2,1)} %param.14, f32[128,2048]{1,0:T(8,128)S(1)} %fusion.19, ...), kind=kOutput, calls=%fused_computation.101 | convolution fusion | flops 539623296 | bytes 6032384 | tf_op jit(solution)/shard_map/dot_general | solution.py:50
  98.6 3.9 %fusion.49 = f32[128,512]{1,0:T(8,128)S(1)} fusion(bf16[2,512,2048]{2,1,0:T(8,128)(2,1)} %param.13, bf16[2,2048,512]{2,1,0:T(8,128)(2,1)} %param.14, f32[128,2048]{1,0:T(8,128)S(1)} %fusion.31, f32[512]{0:T(512)S(1)} %bitcast.180, f32[1,128,512]{2,1,0:T(8,128)S(1)} %copy-done.4, f32[128,512]{1,0:T(8,128)} %get-tuple-element.305, ...), kind=kOutput, calls=%fused_computation.57 | convolution fusion | flops 539754496 | bytes 6294528 | tf_op jit(solution)/shard_map/dot_general | solution.py:50
  102.7 1.8 fusion.133
  104.6 19.1 %all-gather.3 = f32[16,1,512]{2,1,0:T(1,128)S(1)} all-gather(f32[1,1,512]{2,1,0:T(1,128)S(1)} %bitcast.183), channel_id=1, replica_groups=mesh['layer'=16,'dp'=2] {'layer'}, dimensions={0}, use_global_device_ids=true | all-gather | bytes 34816 | tf_op jit(solution)/shard_map/all_gather | solution.py:12
  125.4 28.2 %all-gather.15.cloned.1.call-done = f32[2048,512]{1,0:T(8,128)} async-done(((f32[128,512]{1,0:T(8,128)}), f32[2048,512]{1,0:T(8,128)}) %all-gather.15.cloned.1.call-update) | async-done | bytes 4194320 | tf_op jit(solution)/shard_map/all_gather | solution.py:12
  153.7 19.3 %while.31 = (s32[]{:T(128)}, f32[128,512]{1,0:T(8,128)S(1)}, s32[]{:T(128)}, f32[16,512]{1,0:T(8,128)S(1)}, f32[16,128,512]{2,1,0:T(8,128)}, /*index=5*/s32[]{:T(128)}, s32[]{:T(128)}, s32[]{:T(128)}, s32[]{:T(128)}) while((s32[]{:T(128)}, f32[128,512]{1,0:T(8,128)S(1)}, s32[]{:T(128)}, f32[16,512]{1,0:T(8,128)S(1)}, ...), condition=%wide.region_9.10_spmd.clone, body=%wide.region_8.9_spmd.clone.sunk | while | flops 262152 | bytes 792751 | solution.py:23
  154.9 1.2 fusion.151
  156.1 1.2 fusion.151
  157.3 1.2 fusion.151
  158.5 1.2 fusion.151
  159.7 1.2 fusion.151
  160.9 1.2 fusion.151
  162.1 1.2 fusion.151
  163.3 1.2 fusion.151
  164.6 1.2 fusion.151
  165.8 1.2 fusion.151
  167.0 1.2 fusion.151
  168.2 1.2 fusion.151
  170.6 1.2 fusion.151
  171.8 1.2 fusion.151
  173.0 2.6 %fusion.8 = bf16[128,2048]{1,0:T(8,128)(2,1)S(1)} fusion(bf16[2,2048,512]{2,1,0:T(8,128)(2,1)} %param.14, f32[128,2048]{1,0:T(8,128)S(1)} %fusion.19, f32[128,512]{1,0:T(8,128)S(1)} %get-tuple-element.289), kind=kOutput, calls=%fused_computation.16 | convolution fusion | flops 270925824 | bytes 3932160 | tf_op jit(solution)/shard_map/dot_general | solution.py:46
  180.2 12.6 %all_gather.38 = bf16[2,256,512]{2,1,0:T(8,128)(2,1)S(1)} all-gather(bf16[2,128,512]{2,1,0:T(8,128)(2,1)S(1)} %pad_maximum_fusion.2), channel_id=1, replica_groups=mesh['layer'=16,'dp'=2] {'dp'}, dimensions={1}, use_global_device_ids=true | all-gather | bytes 786432 | tf_op jit(solution)/shard_map/all_gather | solution.py:121
  192.8 8.8 %all_gather.41 = bf16[2,256,512]{2,1,0:T(8,128)(2,1)S(1)} all-gather(bf16[2,128,512]{2,1,0:T(8,128)(2,1)S(1)} %pad_maximum_fusion.3), channel_id=1, replica_groups=mesh['layer'=16,'dp'=2] {'dp'}, dimensions={1}, use_global_device_ids=true | all-gather | bytes 786432 | tf_op jit(solution)/shard_map/all_gather | solution.py:124
  201.6 4.1 %fusion.79 = f32[2,1024,512]{2,1,0:T(8,128)} fusion(bf16[2,256,512]{2,1,0:T(8,128)(2,1)S(1)} %all_gather.41, bf16[2,256,2048]{2,1,0:T(8,128)(2,1)} %all-gather.11.cloned.1.call-done, s32[]{:T(128)S(6)} %select_n.96), kind=kOutput, calls=%fused_computation.69 | convolution fusion | flops 536870912 | bytes 5767172 | tf_op jit(solution)/shard_map/ltf,ltd->lfd/dot_general | solution.py:128
  205.7 22.4 %all-gather.9.cloned.1.call-done = bf16[2,256,2048]{2,1,0:T(8,128)(2,1)} async-done(((bf16[2,128,2048]{2,1,0:T(8,128)(2,1)}), bf16[2,256,2048]{2,1,0:T(8,128)(2,1)}) %all-gather.9.cloned.1.call-update) | async-done | bytes 2097168 | tf_op jit(solution)/shard_map/all_gather | solution.py:122
  228.1 4.4 %fusion.100 = f32[2,256,2048]{2,1,0:T(8,128)} fusion(bf16[2,256,2048]{2,1,0:T(8,128)(2,1)} %all-gather.9.cloned.1.call-done, bf16[2,256,512]{2,1,0:T(8,128)(2,1)S(1)} %all_gather.38, s32[]{:T(128)S(6)} %select_n.95), kind=kOutput, calls=%fused_computation.97 | convolution fusion | flops 536870912 | bytes 6553604 | tf_op jit(solution)/shard_map/ltd,ltf->ldf/dot_general | solution.py:127
  (88 shorter events, 14.0 us)
Async XLA Ops:
  7.2 62.2 %all-gather.13.cloned.1.call-start = ((), (), s32[]{:S(2)}) async-start(), calls=%async_computation.2 | async-start | bytes 4456448 | tf_op jit(solution)/shard_map/all_gather | solution.py:12
  9.1 3.2 %copy-start.6 = (f32[1,512]{1,0:T(1,128)S(1)}, f32[1,512]{1,0:T(1,128)}, u32[]{:S(2)}) copy-start(f32[1,512]{1,0:T(1,128)} %param.15) | copy-start | bytes 6148
  9.1 3.2 %copy-start.3 = (f32[1,128,512]{2,1,0:T(8,128)S(1)}, f32[1,128,512]{2,1,0:T(8,128)}, u32[]{:S(2)}) copy-start(f32[1,128,512]{2,1,0:T(8,128)} %param.10) | copy-start | bytes 786436
  16.1 137.6 %all-gather.15.cloned.1.call-start = ((), (), s32[]{:S(2)}) async-start(), calls=%async_computation.3 | async-start | bytes 4456448 | tf_op jit(solution)/shard_map/all_gather | solution.py:12
  88.5 2.9 %copy-start.7 = (bf16[2,2048,512]{2,1,0:T(8,128)(2,1)S(1)}, bf16[2,2048,512]{2,1,0:T(8,128)(2,1)}, u32[]{:S(2)}) copy-start(bf16[2,2048,512]{2,1,0:T(8,128)(2,1)} %param.14) | copy-start | bytes 12582916
  88.6 14.0 %copy-start = (f32[128,512]{1,0:T(8,128)}, f32[128,512]{1,0:T(8,128)S(1)}, u32[]{:S(2)}) copy-start(f32[128,512]{1,0:T(8,128)S(1)} %get-tuple-element.291) | copy-start | bytes 786436
  91.4 2.2 copy-start.1
  91.4 2.7 %copy-start.4 = (f32[1,128,512]{2,1,0:T(8,128)S(1)}, f32[1,128,512]{2,1,0:T(8,128)}, u32[]{:S(2)}) copy-start(f32[1,128,512]{2,1,0:T(8,128)} %param.11) | copy-start | bytes 786436
  104.5 97.1 %all-gather.11.cloned.1.call-start = ((), (), s32[]{:S(2)}) async-start(), calls=%async_computation.1 | async-start | bytes 3145728 | tf_op jit(solution)/shard_map/all_gather | solution.py:123
  125.4 102.8 %all-gather.9.cloned.1.call-start = ((), (), s32[]{:S(2)}) async-start(), calls=%async_computation | async-start | bytes 3145728 | tf_op jit(solution)/shard_map/all_gather | solution.py:122
  173.0 3.9 %copy-start.5 = (f32[128,512]{1,0:T(8,128)}, f32[128,512]{1,0:T(8,128)S(1)}, u32[]{:S(2)}) copy-start(f32[128,512]{1,0:T(8,128)S(1)} %get-tuple-element.289) | copy-start | bytes 786436
  173.0 2.9 %copy-start.2 = (bf16[2,512,2048]{2,1,0:T(8,128)(2,1)S(1)}, bf16[2,512,2048]{2,1,0:T(8,128)(2,1)}, u32[]{:S(2)}) copy-start(bf16[2,512,2048]{2,1,0:T(8,128)(2,1)} %param.13) | copy-start | bytes 12582916
  175.9 2.2 copy-start.8
Sparse Core Ops, SparseCore 0:
  16.2 53.0 all-gather.12
  104.6 48.9 all-gather.14
  155.8 35.1 all-gather.10
  192.9 35.1 all-gather.8
where the time goes:
time: 240 us; the launch traced here: 239 us
  waiting for transfers between devices  80.6 us (34%)
  blocking collectives  63.9 us (27%)
  other arithmetic  43.3 us (18%)
  matrix products  31.5 us (13%)
  between operations  14 us (6%)
  local copies, waits for them, and re-layouts  4.58 us (2%)
    all_gather x2, waiting for transfers between devices, carried_in(): everything = jax.tree.map(lambda part: lax.all_gather(part, axis), x)  58.1 us
    all_gather x2, blocking collectives, carried_in(): everything = jax.tree.map(lambda part: lax.all_gather(part, axis), x)  42.4 us
    select_n x32, other arithmetic, step(): return jax.tree.map(lambda a, b: jnp.where(reached, a, b), new, before)  37.1 us
    all_gather x1, waiting for transfers between devices, shards(): piece_pre = lax.all_gather(pre_all, 'dp', axis=1, tiled=True)  22.4 us
    all_gather x1, blocking collectives, shards(): piece_normed = lax.all_gather(normed_all, 'dp', axis=1, tiled=True)  12.6 us
    dot_general x3, matrix products, layer_backward(): jnp.dot(pre_grad, up_matrix.T, preferred_element_type=jnp.float32)  9.26 us
    all_gather x1, blocking collectives, shards(): piece_out = lax.all_gather(out_all, 'dp', axis=1, tiled=True)  8.79 us
    dot_general x3, matrix products, layer_forward(): jnp.dot(hidden, down_matrix, preferred_element_type=jnp.float32)  7.55 us
  transfers between devices with their start and end apart: 4, of which 3 were waited for; matrix products, arithmetic and copies ran while one was open for 13% of the time, Pallas kernels for 0%

commit v1 on v0

v1 whole, which is shorter than its diff:
```python
import functools

import jax
import jax.numpy as jnp
from jax import lax
from jax.experimental import pallas as pl
from jax.experimental.pallas import tpu as pltpu
from jax.sharding import PartitionSpec as P

eps = 1e-06
step_length = 0.5
MESH = pl.DeviceIdType.MESH
F32 = jnp.float32
BF16 = jnp.bfloat16


def dot(a, b):
    return jnp.dot(a, b, preferred_element_type=F32)


def dot_t(a, b):
    return lax.dot_general(a, b, (((1,), (1,)), ((), ())), preferred_element_type=F32)


def unit_of(state):
    r = lax.rsqrt(jnp.mean(state * state, axis=-1, keepdims=True) + eps)
    return state * r, r


def kernel(
    n, group, tile,
    guess_ref, adj_ref, gain_ref, rate_ref, up_hbm, down_hbm,
    point_ref, adjoint_ref, normed_ref, pre_ref, hidden_ref, outg_ref,
    up, down, slope, acc, states, operand,
    rates, shift_out, shift_in, part_out, part_in, cross_out, cross_in,
    w_sem, rate_send, rate_recv, shift_send, shift_recv, part_send, part_recv,
    cross_send, cross_recv,
):
    me = lax.axis_index("layer")
    mine = lax.axis_index("dp")
    layers, width, ff = up.shape
    tokens = guess_ref.shape[0]
    share = tokens // n
    tiles = ff // tile

    barrier = pltpu.get_barrier_semaphore()

    @pl.loop(1, n)
    def _(d):
        pl.semaphore_signal(
            barrier, inc=1, device_id={"layer": lax.rem(me + d, n)}, device_id_type=MESH
        )

    for q in range(1, group):
        pl.semaphore_signal(
            barrier, inc=1, device_id={"dp": lax.rem(mine + q, group)}, device_id_type=MESH
        )

    loads = []
    for l in range(layers):
        loads.append(
            (
                pltpu.make_async_copy(up_hbm.at[l], up.at[l], w_sem.at[2 * l]),
                pltpu.make_async_copy(down_hbm.at[l], down.at[l], w_sem.at[2 * l + 1]),
            )
        )
    for a, b in loads:
        a.start()
        b.start()

    def columns(f):
        return pl.ds(pl.multiple_of(f * tile, tile), tile)

    def forward(l, state, slot, with_down, before_down=None):
        unit, _ = unit_of(state)
        normed = (unit * gain_ref[pl.ds(l, 1), :]).astype(BF16)
        operand[...] = normed
        if slot is not None:
            normed_ref[l, slot] = normed
        acc[...] = jnp.zeros_like(acc)

        @pl.loop(0, tiles)
        def _(f):
            cols = columns(f)
            preact = dot(operand[...], up[l, :, cols])
            s = 0.5 + 0.5 * jnp.tanh(0.5 * preact)
            hidden = (preact * s).astype(BF16)
            if slot is not None:
                hidden_ref[l, slot, :, cols] = hidden
                slope[l, slot, :, cols] = s * (1.0 + preact * (1.0 - s))
            if with_down:
                acc[...] += dot(hidden, down[l, cols, :])

        return state + step_length * acc[...]

    def backward(l, state, cotangent, slot, keep, with_input):
        out_grad = (step_length * cotangent).astype(BF16)
        operand[...] = out_grad
        if keep:
            outg_ref[l, slot] = out_grad
        acc[...] = jnp.zeros_like(acc)

        @pl.loop(0, tiles)
        def _(f):
            cols = columns(f)
            pre = (dot_t(operand[...], down[l, cols, :]) * slope[l, slot, :, cols]).astype(BF16)
            if keep:
                pre_ref[l, slot, :, cols] = pre
            if with_input:
                acc[...] += dot_t(pre, up[l, :, cols])

        if not with_input:
            return None
        unit, r = unit_of(state)
        unit_grad = acc[...] * gain_ref[pl.ds(l, 1), :]
        inner = jnp.mean(unit_grad * unit, axis=-1, keepdims=True)
        return cotangent + r * (unit_grad - unit * inner)

    def block_inputs(start, slot):
        states[slot, 0] = start
        state = start
        for l in range(layers):
            state = forward(l, state, slot, l < layers - 1)
            if l < layers - 1:
                states[slot, l + 1] = state

    def block_backward(cotangent, slot, keep):
        for l in reversed(range(layers)):
            cotangent = backward(
                l, states[slot, l], cotangent, slot, keep, l > 0 or not keep
            )
        return cotangent

    def exchange(src, dst, send, recv, src_at, peer):
        return pltpu.make_async_remote_copy(
            src_ref=src.at[src_at],
            dst_ref=dst.at[me],
            send_sem=send.at[peer],
            recv_sem=recv.at[me],
            device_id={"layer": peer},
            device_id_type=MESH,
        )

    def arrival(src, dst, send, recv, peer):
        return pltpu.make_async_remote_copy(
            src_ref=src.at[peer],
            dst_ref=dst.at[peer],
            send_sem=send.at[peer],
            recv_sem=recv.at[peer],
            device_id={"layer": peer},
            device_id_type=MESH,
        )

    def start_sweep(phase, shift):
        src, dst = shift_out.at[phase], shift_in.at[phase]
        for k in range(n):
            src[k] = shift[k * share : (k + 1) * share].astype(BF16)
        dst[me] = src[me]

        @pl.loop(1, n)
        def _(d):
            peer = lax.rem(me + d, n)
            exchange(src, dst, shift_send.at[phase], shift_recv.at[phase], peer, peer).start()

    def finish_sweep(phase, reverse, out):
        src, dst = shift_out.at[phase], shift_in.at[phase]
        psrc, pdst = part_out.at[phase], part_in.at[phase]

        def step(k, before):
            j = n - 1 - k if reverse else k
            psrc[j] = before.astype(BF16)

            @pl.when(j == me)
            def _():
                pdst[j] = before.astype(BF16)

            @pl.when(j != me)
            def _():
                exchange(psrc, pdst, part_send.at[phase], part_recv.at[phase], j, j).start()
                arrival(src, dst, shift_send.at[phase], shift_recv.at[phase], j).wait_recv()
                if phase == 0:
                    arrival(rates, rates, rate_send, rate_recv, j).wait_recv()

            here = dst[j].astype(F32)
            return jnp.where(k == 0, here, here + rates[j] * before)

        lax.fori_loop(0, n, step, jnp.zeros((share, width), F32))

        @pl.loop(1, n)
        def _(d):
            peer = lax.rem(me + d, n)
            arrival(psrc, pdst, part_send.at[phase], part_recv.at[phase], peer).wait_recv()

        for k in range(n):
            out[k * share : (k + 1) * share, :] = pdst[k].astype(F32)

    def cross(phase, q):
        peer = lax.rem(mine + q, group)
        return pltpu.make_async_remote_copy(
            src_ref=cross_out.at[phase],
            dst_ref=cross_in.at[phase, q - 1],
            send_sem=cross_send.at[phase, q - 1],
            recv_sem=cross_recv.at[phase, q - 1],
            device_id={"dp": peer},
            device_id_type=MESH,
        )

    rates[me] = rate_ref[...]
    guess = guess_ref[...]
    state = guess
    for l in range(layers):
        loads[l][0].wait()
        loads[l][1].wait()
        state = forward(l, state, None, True)
        if l == 0:
            pl.semaphore_wait(barrier, n - 1 + group - 1)

            @pl.loop(1, n)
            def _(d):
                peer = lax.rem(me + d, n)
                exchange(rates, rates, rate_send, rate_recv, me, peer).start()

    shift = state - jnp.where(me == 0, 0.0, 1.0) * (rate_ref[...] * guess)
    start_sweep(0, shift)
    finish_sweep(0, False, point_ref)

    @pl.when(me == 0)
    def _():
        point_ref[...] = guess_ref[...]

    cross_out[0] = point_ref[...].astype(BF16)
    for q in range(1, group):
        cross(0, q).start()

    block_inputs(point_ref[...], 0)
    begin = block_backward(adj_ref[...], 0, False)
    shift = begin - jnp.where(me == n - 1, 0.0, 1.0) * (rate_ref[...] * adj_ref[...])
    start_sweep(1, shift)
    for q in range(1, group):
        cross(0, q).wait_recv()
        block_inputs(cross_in[0, q - 1].astype(F32), q)
    finish_sweep(1, True, adjoint_ref)

    @pl.when(me == n - 1)
    def _():
        adjoint_ref[...] = adj_ref[...]

    cross_out[1] = adjoint_ref[...].astype(BF16)
    for q in range(1, group):
        cross(1, q).start()
    block_backward(adjoint_ref[...], 0, True)
    for q in range(1, group):
        cross(1, q).wait_recv()
        block_backward(cross_in[1, q - 1].astype(F32), q, True)

    for q in range(1, group):
        cross(0, q).wait_send()
        cross(1, q).wait_send()

    @pl.loop(1, n)
    def _(d):
        peer = lax.rem(me + d, n)
        arrival(rates, rates, rate_send, rate_recv, peer).wait_send()
        for phase in range(2):
            arrival(
                shift_out.at[phase], shift_in.at[phase],
                shift_send.at[phase], shift_recv.at[phase], peer,
            ).wait_send()
            arrival(
                part_out.at[phase], part_in.at[phase],
                part_send.at[phase], part_recv.at[phase], peer,
            ).wait_send()


def relax(c_guess, adj_guess, gain, rate, ups, downs):
    n, group = lax.axis_size("layer"), lax.axis_size("dp")
    tokens, width = c_guess.shape
    layers, _, ff = ups.shape
    tile = min(ff, 512)
    share = tokens // n
    vmem = pl.BlockSpec(memory_space=pltpu.VMEM)
    hbm = pl.BlockSpec(memory_space=pl.ANY)
    dma = pltpu.SemaphoreType.DMA
    return pl.pallas_call(
        functools.partial(kernel, n, group, tile),
        out_shape=(
            jax.ShapeDtypeStruct((tokens, width), F32),
            jax.ShapeDtypeStruct((tokens, width), F32),
            jax.ShapeDtypeStruct((layers, group, tokens, width), BF16),
            jax.ShapeDtypeStruct((layers, group, tokens, ff), BF16),
            jax.ShapeDtypeStruct((layers, group, tokens, ff), BF16),
            jax.ShapeDtypeStruct((layers, group, tokens, width), BF16),
        ),
        in_specs=[vmem, vmem, vmem, vmem, hbm, hbm],
        out_specs=(vmem,) * 6,
        scratch_shapes=[
            pltpu.VMEM((layers, width, ff), BF16),
            pltpu.VMEM((layers, ff, width), BF16),
            pltpu.VMEM((layers, group, tokens, ff), F32),
            pltpu.VMEM((tokens, width), F32),
            pltpu.VMEM((group, layers, tokens, width), F32),
            pltpu.VMEM((tokens, width), BF16),
            pltpu.VMEM((n, 1, width), F32),
            pltpu.VMEM((2, n, share, width), BF16),
            pltpu.VMEM((2, n, share, width), BF16),
            pltpu.VMEM((2, n, share, width), BF16),
            pltpu.VMEM((2, n, share, width), BF16),
            pltpu.VMEM((2, tokens, width), BF16),
            pltpu.VMEM((2, max(group - 1, 1), tokens, width), BF16),
            dma((2 * layers,)),
            dma((n,)), dma((n,)),
            dma((2, n)), dma((2, n)),
            dma((2, n)), dma((2, n)),
            dma((2, max(group - 1, 1))), dma((2, max(group - 1, 1))),
        ],
        compiler_params=pltpu.CompilerParams(
            collective_id=0, has_side_effects=True, vmem_limit_bytes=60 * 2**20
        ),
    )(c_guess, adj_guess, gain, rate, ups, downs)


def shards(c_guess, adj_guess, norm_gain, w_up, w_down, coarse_rate):
    group = lax.axis_size("dp")
    member = lax.axis_index("dp")
    point, adjoint, normed, pre, hidden, outg = relax(
        c_guess[0], adj_guess[0], norm_gain, coarse_rate, w_up, w_down
    )
    flat = lambda x: x.reshape(x.shape[0], -1, x.shape[-1])
    normed, pre, hidden, outg = map(flat, (normed, pre, hidden, outg))
    width_share = w_up.shape[1] // group
    hidden_share = w_up.shape[2] // group
    normed_cols = lax.dynamic_slice_in_dim(normed, member * width_share, width_share, 2)
    hidden_cols = lax.dynamic_slice_in_dim(hidden, member * hidden_share, hidden_share, 2)
    up_part = jnp.einsum("ltd,ltf->ldf", normed_cols, pre, preferred_element_type=F32)
    down_part = jnp.einsum("ltf,ltd->lfd", hidden_cols, outg, preferred_element_type=F32)
    return (point[None], adjoint[None], up_part, down_part)


def solution(mesh):
    return jax.shard_map(
        shards,
        mesh=mesh,
        in_specs=(
            P("layer", "dp", None),
            P("layer", "dp", None),
            P("layer", None),
            P("layer", None, None),
            P("layer", None, None),
            P("layer", None),
        ),
        out_specs=(
            P("layer", "dp", None),
            P("layer", "dp", None),
            P("layer", "dp", None),
            P("layer", "dp", None),
        ),
        check_vma=False,
    )
```

time: 240 us -> 60.5 us (0.25)
  waiting for transfers between devices: 80.6 us -> 0 us
  blocking collectives: 63.9 us -> 0 us
  Pallas kernels: 0 us -> 50.9 us
  other arithmetic: 43.3 us -> 0 us
  matrix products: 31.5 us -> 7.38 us
  between operations: 14 us -> 0.68 us
  local copies, waits for them, and re-layouts: 4.58 us -> 1.42 us
    all_gather x4 -> x0, waiting for transfers between devices: 80.5 us -> none  [the longest x2 58.1 us: carried_in(): everything = jax.tree.map(lambda part: lax.all_gather(part, axis), x)]
    all_gather x4 -> x0, blocking collectives: 63.9 us -> none  [the longest x2 42.4 us: carried_in(): everything = jax.tree.map(lambda part: lax.all_gather(part, axis), x)]
    pallas_call x0 -> x1, Pallas kernels: none -> 50.9 us  [relax(): pl.pallas_call(functools.partial(kernel, n, group, tile), out_shape=(jax....]
    select_n x33 -> x0, other arithmetic: 37.1 us -> none  [the longest x32 37.1 us: step(): return jax.tree.map(lambda a, b: jnp.where(reached, a, b), new, before)]
    dot_general x12 -> x2, matrix products: 31.5 us -> 7.38 us  [the longest x1 4.6 us: shards(): jnp.einsum('ltd,ltf->ldf', normed_cols, pre, preferred_element_type=F32)]
    another operation x8 -> x0, other arithmetic: 4.81 us -> none  [the longest x3 2.05 us: block_backward(): jnp.stack(normed_list)]
  transfers between devices with their start and end apart: 4 -> 0, of which waited for: 3 -> 0; matrix products, arithmetic and copies ran while one was open for 13% -> 0% of each run, Pallas kernels for 0% -> 0%
where the time goes in v1:
time: 60.5 us; the launch traced here: 60.3 us
  Pallas kernels  50.9 us (84%)
  matrix products  7.38 us (12%)
  local copies, waits for them, and re-layouts  1.42 us (2%)
  between operations  0.68 us (1%)
    pallas_call x1, Pallas kernels, relax(): pl.pallas_call(functools.partial(kernel, n, group, tile), out_shape=(jax....  50.9 us
    dot_general x1, matrix products, shards(): jnp.einsum('ltd,ltf->ldf', normed_cols, pre, preferred_element_type=F32)  4.6 us
    dot_general x1, matrix products, shards(): jnp.einsum('ltf,ltd->lfd', hidden_cols, outg, preferred_element_type=F32)  2.78 us
    unnamed x10, local copies, waits for them, and re-layouts  1.42 us

profile of v1, /device:TPU:0, one launch (start us, length us, event | category | flops | bytes accessed | tf_op | source)
XLA Modules:
  0.0 60.3 jit_solution(9231787005932205117)
XLA Ops:
  0.6 50.9 %shard_map.93 = (f32[128,512]{1,0:T(8,128)}, f32[128,512]{1,0:T(8,128)}, bf16[2,2,128,512]{3,2,1,0:T(8,128)(2,1)}, bf16[2,2,128,2048]{3,2,1,0:T(8,128)(2,1)}, bf...) custom-call(f32[128,512]{1,0:T(8,128)} %bitcast.13, f32[128,512]{1,0:T(8,128)} %bitcast.14, ...), custom_call_target="tpu_custom_call" | custom-call | tf_op jit(solution)/shard_map/pallas_call | solution.py:284
  51.5 0.0 copy-start
  51.5 0.0 copy-start.1
  51.5 4.6 %fusion.2 = f32[2,256,2048]{2,1,0:T(8,128)} fusion(bf16[2,256,2048]{2,1,0:T(8,128)(2,1)} %bitcast.10, bf16[2,256,512]{2,1,0:T(8,128)(2,1)} %bitcast.17, s32[]{:T(128)S(6)} %select_n.6), kind=kOutput, calls=%fused_computation.2 | convolution fusion | flops 536870912 | bytes 6553604 | tf_op jit(solution)/shard_map/ltd,ltf->ldf/dot_general | solution.py:334
  56.1 0.0 copy-done
  56.1 0.0 copy-done.1
  56.1 0.0 copy-start.3
  56.1 0.0 copy-start.2
  56.1 2.8 %fusion = f32[2,1024,512]{2,1,0:T(8,128)} fusion(bf16[2,256,512]{2,1,0:T(8,128)(2,1)S(1)} %bitcast.11, bf16[2,256,2048]{2,1,0:T(8,128)(2,1)S(1)} %bitcast.12, s32[]{:T(128)S(6)} %select_n.7), kind=kOutput, calls=%fused_computation | convolution fusion | flops 536870912 | bytes 5767172 | tf_op jit(solution)/shard_map/ltf,ltd->lfd/dot_general | solution.py:335
  58.9 0.0 copy-done.3
  58.9 0.7 %copy.16 = f32[1,128,512]{2,1,0:T(8,128)} copy(f32[1,128,512]{2,1,0:T(8,128)S(1)} %bitcast.16) | data formatting | bytes 524288
  59.6 0.0 copy-done.2
  59.6 0.7 %copy.17 = f32[1,128,512]{2,1,0:T(8,128)} copy(f32[1,128,512]{2,1,0:T(8,128)S(1)} %bitcast.15) | data formatting | bytes 524288
Async XLA Ops:
  51.5 4.6 %copy-start = (bf16[2,2,128,512]{3,2,1,0:T(8,128)(2,1)S(1)}, bf16[2,2,128,512]{3,2,1,0:T(8,128)(2,1)}, u32[]{:S(2)}) copy-start(bf16[2,2,128,512]{3,2,1,0:T(8,128)(2,1)} %get-tuple-element.15) | copy-start | bytes 1572868
  51.5 4.6 %copy-start.1 = (bf16[2,2,128,2048]{3,2,1,0:T(8,128)(2,1)S(1)}, bf16[2,2,128,2048]{3,2,1,0:T(8,128)(2,1)}, u32[]{:S(2)}) copy-start(bf16[2,2,128,2048]{3,2,1,0:T(8,128)(2,1)} %get-tuple-element.14) | copy-start | bytes 6291460
  56.1 2.8 %copy-start.3 = (f32[128,512]{1,0:T(8,128)S(1)}, f32[128,512]{1,0:T(8,128)}, u32[]{:S(2)}) copy-start(f32[128,512]{1,0:T(8,128)} %get-tuple-element.10) | copy-start | bytes 786436
  56.1 3.5 %copy-start.2 = (f32[128,512]{1,0:T(8,128)S(1)}, f32[128,512]{1,0:T(8,128)}, u32[]{:S(2)}) copy-start(f32[128,512]{1,0:T(8,128)} %get-tuple-element.11) | copy-start | bytes 786436

commit v2 on v1

--- a/solution.py
+++ b/solution.py
@@ -28,13 +28,14 @@
 
 
 def kernel(
-    n, group, tile,
+    n, group, tile, sliced,
     guess_ref, adj_ref, gain_ref, rate_ref, up_hbm, down_hbm,
+    point_out, adjoint_out, normed_out, pre_out, hidden_out, outg_out,
     point_ref, adjoint_ref, normed_ref, pre_ref, hidden_ref, outg_ref,
     up, down, slope, acc, states, operand,
-    rates, shift_out, shift_in, part_out, part_in, cross_out, cross_in,
+    rates, shift_out, shift_in, part_out, part_in, cross_out, cross_in, staged,
     w_sem, rate_send, rate_recv, shift_send, shift_recv, part_send, part_recv,
-    cross_send, cross_recv,
+    cross_send, cross_recv, end_sem, in_sem, back_sem,
 ):
     me = lax.axis_index("layer")
     mine = lax.axis_index("dp")
@@ -42,6 +43,17 @@
     tokens = guess_ref.shape[0]
     share = tokens // n
     tiles = ff // tile
+    wcols = width // group
+    per = max(tiles // group, 1)
+    ends = []
+
+    def put(src, dst, sem):
+        copy = pltpu.make_async_copy(src, dst, sem)
+        copy.start()
+        ends.append(copy)
+
+    cross_out[0] = guess_ref[...].astype(BF16).reshape(n, share, width)
+    cross_out[1] = adj_ref[...].astype(BF16).reshape(n, share, width)
 
     barrier = pltpu.get_barrier_semaphore()
 
@@ -76,7 +88,10 @@
         normed = (unit * gain_ref[pl.ds(l, 1), :]).astype(BF16)
         operand[...] = normed
         if slot is not None:
-            normed_ref[l, slot] = normed
+            if sliced:
+                normed_ref[l, slot] = operand[:, pl.ds(pl.multiple_of(mine * wcols, 128), wcols)]
+            else:
+                normed_ref[l, slot] = normed
         acc[...] = jnp.zeros_like(acc)
 
         @pl.loop(0, tiles)
@@ -86,7 +101,12 @@
             s = 0.5 + 0.5 * jnp.tanh(0.5 * preact)
             hidden = (preact * s).astype(BF16)
             if slot is not None:
-                hidden_ref[l, slot, :, cols] = hidden
+                if sliced:
+                    @pl.when(lax.div(f, per) == mine)
+                    def _():
+                        hidden_ref[l, slot, :, columns(lax.rem(f, per))] = hidden
+                else:
+                    hidden_ref[l, slot, :, cols] = hidden
                 slope[l, slot, :, cols] = s * (1.0 + preact * (1.0 - s))
             if with_down:
                 acc[...] += dot(hidden, down[l, cols, :])
@@ -123,12 +143,17 @@
             state = forward(l, state, slot, l < layers - 1)
             if l < layers - 1:
                 states[slot, l + 1] = state
+        put(normed_ref.at[:, slot], normed_out.at[:, slot], in_sem.at[slot, 0])
+        put(hidden_ref.at[:, slot], hidden_out.at[:, slot], in_sem.at[slot, 1])
 
     def block_backward(cotangent, slot, keep):
         for l in reversed(range(layers)):
             cotangent = backward(
                 l, states[slot, l], cotangent, slot, keep, l > 0 or not keep
             )
+            if keep:
+                put(outg_ref.at[l, slot], outg_out.at[l, slot], back_sem.at[l, slot, 0])
+                put(pre_ref.at[l, slot], pre_out.at[l, slot], back_sem.at[l, slot, 1])
         return cotangent
 
     def exchange(src, dst, send, recv, src_at, peer):
@@ -186,41 +211,73 @@
 
         lax.fori_loop(0, n, step, jnp.zeros((share, width), F32))
 
+        edge = n - 1 if reverse else 0
+
+        def pass_on(k):
+            @pl.when(me == edge)
+            def _():
+                for q in range(1, group):
+                    cross(phase, q, cross_out.at[phase], k).start()
+
+            @pl.when(me != edge)
+            def _():
+                for q in range(1, group):
+                    cross(phase, q, pdst, k).start()
+
+        pass_on(me)
+
         @pl.loop(1, n)
         def _(d):
             peer = lax.rem(me + d, n)
             arrival(psrc, pdst, part_send.at[phase], part_recv.at[phase], peer).wait_recv()
+            pass_on(peer)
 
         for k in range(n):
             out[k * share : (k + 1) * share, :] = pdst[k].astype(F32)
 
-    def cross(phase, q):
+    def cross(phase, q, src, k):
         peer = lax.rem(mine + q, group)
         return pltpu.make_async_remote_copy(
-            src_ref=cross_out.at[phase],
-            dst_ref=cross_in.at[phase, q - 1],
-            send_sem=cross_send.at[phase, q - 1],
-            recv_sem=cross_recv.at[phase, q - 1],
+            src_ref=src.at[k],
+            dst_ref=cross_in.at[phase, q - 1, k],
+            send_sem=cross_send.at[phase, q - 1, k],
+            recv_sem=cross_recv.at[phase, q - 1, k],
             device_id={"dp": peer},
             device_id_type=MESH,
         )
+
+    def crossed(phase, q):
+        @pl.loop(0, n)
+        def _(k):
+            cross(phase, q, cross_out.at[phase], k).wait_recv()
+
+        for k in range(n):
+            staged[k * share : (k + 1) * share, :] = cross_in[phase, q - 1, k].astype(F32)
+        return staged[...]
 
     rates[me] = rate_ref[...]
     guess = guess_ref[...]
     state = guess
-    for l in range(layers):
-        loads[l][0].wait()
-        loads[l][1].wait()
-        state = forward(l, state, None, True)
-        if l == 0:
-            pl.semaphore_wait(barrier, n - 1 + group - 1)
-
-            @pl.loop(1, n)
-            def _(d):
-                peer = lax.rem(me + d, n)
-                exchange(rates, rates, rate_send, rate_recv, me, peer).start()
-
-    shift = state - jnp.where(me == 0, 0.0, 1.0) * (rate_ref[...] * guess)
+    for copies in loads:
+        for copy in copies:
+            copy.wait()
+    staged[...] = jnp.zeros_like(staged)
+
+    @pl.when(me < n - 1)
+    def _():
+        state = guess
+        for l in range(layers):
+            state = forward(l, state, None, True)
+        staged[...] = state
+
+    pl.semaphore_wait(barrier, n - 1 + group - 1)
+
+    @pl.loop(1, n)
+    def _(d):
+        peer = lax.rem(me + d, n)
+        exchange(rates, rates, rate_send, rate_recv, me, peer).start()
+
+    shift = staged[...] - jnp.where(me == 0, 0.0, 1.0) * (rate_ref[...] * guess)
     start_sweep(0, shift)
     finish_sweep(0, False, point_ref)
 
@@ -228,34 +285,29 @@
     def _():
         point_ref[...] = guess_ref[...]
 
-    cross_out[0] = point_ref[...].astype(BF16)
-    for q in range(1, group):
-        cross(0, q).start()
-
+    put(point_ref, point_out, end_sem.at[0])
     block_inputs(point_ref[...], 0)
     begin = block_backward(adj_ref[...], 0, False)
     shift = begin - jnp.where(me == n - 1, 0.0, 1.0) * (rate_ref[...] * adj_ref[...])
     start_sweep(1, shift)
     for q in range(1, group):
-        cross(0, q).wait_recv()
-        block_inputs(cross_in[0, q - 1].astype(F32), q)
+        block_inputs(crossed(0, q), q)
     finish_sweep(1, True, adjoint_ref)
 
     @pl.when(me == n - 1)
     def _():
         adjoint_ref[...] = adj_ref[...]
 
-    cross_out[1] = adjoint_ref[...].astype(BF16)
-    for q in range(1, group):
-        cross(1, q).start()
+    put(adjoint_ref, adjoint_out, end_sem.at[1])
     block_backward(adjoint_ref[...], 0, True)
     for q in range(1, group):
-        cross(1, q).wait_recv()
-        block_backward(cross_in[1, q - 1].astype(F32), q, True)
+        block_backward(crossed(1, q), q, True)
 
     for q in range(1, group):
-        cross(0, q).wait_send()
-        cross(1, q).wait_send()
+        @pl.loop(0, n)
+        def _(k):
+            for phase in range(2):
+                cross(phase, q, cross_out.at[phase], k).wait_send()
 
     @pl.loop(1, n)
     def _(d):
@@ -271,6 +323,9 @@
                 part_send.at[phase], part_recv.at[phase], peer,
             ).wait_send()
 
+    for copy in ends:
+        copy.wait()
+
 
 def relax(c_guess, adj_guess, gain, rate, ups, downs):
     n, group = lax.axis_size("layer"), lax.axis_size("dp")
@@ -278,22 +333,32 @@
     layers, _, ff = ups.shape
     tile = min(ff, 512)
     share = tokens // n
+    sliced = (width // group) % 128 == 0 and (ff // group) % tile == 0
+    wcols = width // group if sliced else width
+    fcols = ff // group if sliced else ff
     vmem = pl.BlockSpec(memory_space=pltpu.VMEM)
     hbm = pl.BlockSpec(memory_space=pl.ANY)
     dma = pltpu.SemaphoreType.DMA
+    others = max(group - 1, 1)
     return pl.pallas_call(
-        functools.partial(kernel, n, group, tile),
+        functools.partial(kernel, n, group, tile, sliced),
         out_shape=(
             jax.ShapeDtypeStruct((tokens, width), F32),
             jax.ShapeDtypeStruct((tokens, width), F32),
+            jax.ShapeDtypeStruct((layers, group, tokens, wcols), BF16),
+            jax.ShapeDtypeStruct((layers, group, tokens, ff), BF16),
+            jax.ShapeDtypeStruct((layers, group, tokens, fcols), BF16),
             jax.ShapeDtypeStruct((layers, group, tokens, width), BF16),
-            jax.ShapeDtypeStruct((layers, group, tokens, ff), BF16),
-            jax.ShapeDtypeStruct((layers, group, tokens, ff), BF16),
-            jax.ShapeDtypeStruct((layers, group, tokens, width), BF16),
         ),
         in_specs=[vmem, vmem, vmem, vmem, hbm, hbm],
-        out_specs=(vmem,) * 6,
+        out_specs=(hbm,) * 6,
         scratch_shapes=[
+            pltpu.VMEM((tokens, width), F32),
+            pltpu.VMEM((tokens, width), F32),
+            pltpu.VMEM((layers, group, tokens, wcols), BF16),
+            pltpu.VMEM((layers, group, tokens, ff), BF16),
+            pltpu.VMEM((layers, group, tokens, fcols), BF16),
+            pltpu.VMEM((layers, group, tokens, width), BF16),
             pltpu.VMEM((layers, width, ff), BF16),
             pltpu.VMEM((layers, ff, width), BF16),
             pltpu.VMEM((layers, group, tokens, ff), F32),
@@ -305,18 +370,66 @@
             pltpu.VMEM((2, n, share, width), BF16),
             pltpu.VMEM((2, n, share, width), BF16),
             pltpu.VMEM((2, n, share, width), BF16),
-            pltpu.VMEM((2, tokens, width), BF16),
-            pltpu.VMEM((2, max(group - 1, 1), tokens, width), BF16),
+            pltpu.VMEM((2, n, share, width), BF16),
+            pltpu.VMEM((2, others, n, share, width), BF16),
+            pltpu.VMEM((tokens, width), F32),
             dma((2 * layers,)),
             dma((n,)), dma((n,)),
             dma((2, n)), dma((2, n)),
             dma((2, n)), dma((2, n)),
-            dma((2, max(group - 1, 1))), dma((2, max(group - 1, 1))),
+            dma((2, others, n)), dma((2, others, n)),
+            dma((2,)), dma((group, 2)), dma((layers, group, 2)),
         ],
         compiler_params=pltpu.CompilerParams(
             collective_id=0, has_side_effects=True, vmem_limit_bytes=60 * 2**20
         ),
     )(c_guess, adj_guess, gain, rate, ups, downs)
+
+
+def gradients_kernel(
+    normed, pre, hidden, outg, point, adjoint, up_part, down_part, point_out, adjoint_out
+):
+    def outer(a, b):
+        return lax.dot_general(a, b, (((0,), (0,)), ((), ())), preferred_element_type=F32)
+
+    up_part[0] = outer(normed[0], pre[0])
+    down_part[0] = outer(hidden[0], outg[0])
+    point_out[...] = point[...]
+    adjoint_out[...] = adjoint[...]
+
+
+def gradients(normed, pre, hidden, outg, point, adjoint):
+    layers, tokens, wcols = normed.shape
+    fcols, ff, width = hidden.shape[2], pre.shape[2], outg.shape[2]
+    cuts = 4 if fcols % 512 == 0 and ff % 512 == 0 else 1
+    rows = point.shape[0] // (layers * cuts)
+    by_layer = lambda l, f: (l, 0, 0)
+    by_cut = lambda l, f: (l, 0, f)
+    by_row = lambda l, f: (l * cuts + f, 0)
+    return pl.pallas_call(
+        gradients_kernel,
+        grid=(layers, cuts),
+        out_shape=(
+            jax.ShapeDtypeStruct((layers, wcols, ff), F32),
+            jax.ShapeDtypeStruct((layers, fcols, width), F32),
+            jax.ShapeDtypeStruct(point.shape, F32),
+            jax.ShapeDtypeStruct(adjoint.shape, F32),
+        ),
+        in_specs=[
+            pl.BlockSpec((1, tokens, wcols), by_layer),
+            pl.BlockSpec((1, tokens, ff // cuts), by_cut),
+            pl.BlockSpec((1, tokens, fcols // cuts), by_cut),
+            pl.BlockSpec((1, tokens, width), by_layer),
+            pl.BlockSpec((rows, width), by_row),
+            pl.BlockSpec((rows, width), by_row),
+        ],
+        out_specs=(
+            pl.BlockSpec((1, wcols, ff // cuts), by_cut),
+            pl.BlockSpec((1, fcols // cuts, width), lambda l, f: (l, f, 0)),
+            pl.BlockSpec((rows, width), by_row),
+            pl.BlockSpec((rows, width), by_row),
+        ),
+    )(normed, pre, hidden, outg, point, adjoint)
 
 
 def shards(c_guess, adj_guess, norm_gain, w_up, w_down, coarse_rate):
@@ -329,10 +442,10 @@
     normed, pre, hidden, outg = map(flat, (normed, pre, hidden, outg))
     width_share = w_up.shape[1] // group
     hidden_share = w_up.shape[2] // group
-    normed_cols = lax.dynamic_slice_in_dim(normed, member * width_share, width_share, 2)
-    hidden_cols = lax.dynamic_slice_in_dim(hidden, member * hidden_share, hidden_share, 2)
-    up_part = jnp.einsum("ltd,ltf->ldf", normed_cols, pre, preferred_element_type=F32)
-    down_part = jnp.einsum("ltf,ltd->lfd", hidden_cols, outg, preferred_element_type=F32)
+    if normed.shape[2] != width_share:
+        normed = lax.dynamic_slice_in_dim(normed, member * width_share, width_share, 2)
+        hidden = lax.dynamic_slice_in_dim(hidden, member * hidden_share, hidden_share, 2)
+    up_part, down_part, point, adjoint = gradients(normed, pre, hidden, outg, point, adjoint)
     return (point[None], adjoint[None], up_part, down_part)
 
 

time: 60.5 us -> 60.8 us (level)
  Pallas kernels: 50.9 us -> 59.8 us
  matrix products: 7.38 us -> 0 us
  local copies, waits for them, and re-layouts: 1.42 us -> 0 us
    pallas_call x1 -> x2, Pallas kernels: 50.9 us -> 59.8 us  [the longest x1 51.4 us: relax(): pl.pallas_call(functools.partial(kernel, n, group, tile, sliced), out_sha...]
    dot_general x2 -> x0, matrix products: 7.38 us -> none  [the longest x1 4.6 us: shards(): jnp.einsum('ltd,ltf->ldf', normed_cols, pre, preferred_element_type=F32)]
    unnamed x10 -> x0, local copies, waits for them, and re-layouts: 1.42 us -> none
where the time goes in v2:
time: 60.8 us; the launch traced here: 60.5 us
  Pallas kernels  59.8 us (98%)
  between operations  0.64 us (1%)
    pallas_call x1, Pallas kernels, relax(): pl.pallas_call(functools.partial(kernel, n, group, tile, sliced), out_sha...  51.4 us
    pallas_call x1, Pallas kernels, gradients(): pl.pallas_call(gradients_kernel, grid=(layers, cuts), out_shape=(jax.Shap...  8.37 us

profile of v2, /device:TPU:0, one launch (start us, length us, event | category | flops | bytes accessed | tf_op | source)
XLA Modules:
  0.0 60.5 jit_solution(9033527861633212803)
XLA Ops:
  0.6 51.4 %shard_map.93 = (f32[128,512]{1,0:T(8,128)}, f32[128,512]{1,0:T(8,128)}, bf16[2,2,128,256]{3,2,1,0:T(8,128)(2,1)}, bf16[2,2,128,2048]{3,2,1,0:T(8,128)(2,1)}, bf...) custom-call(f32[128,512]{1,0:T(8,128)} %bitcast.11, f32[128,512]{1,0:T(8,128)} %bitcast.12, ...), custom_call_target="tpu_custom_call" | custom-call | tf_op jit(solution)/shard_map/pallas_call | solution.py:343
  52.1 8.4 %shard_map.94 = (f32[2,256,2048]{2,1,0:T(8,128)}, f32[2,1024,512]{2,1,0:T(8,128)}, f32[128,512]{1,0:T(8,128)}, f32[128,512]{1,0:T(8,128)}) custom-call(bf16[2,256,256]{2,1,0:T(8,128)(2,1)} %bitcast.13, bf16[2,256,2048]{2,1,0:T(8,128)(2,1)} %bitcast.8, bf16[2,256,1024]{2,1,0:T(8,128)(2,1)} %bitcast.9, bf16[2,256,512]{2,1,0:T(8,128)(2,1)} %bitcast.10, ...), custom_call_target="tpu_custom_call" | custom-call | tf_op jit(solution)/shard_map/pallas_call | solution.py:409

commit v3 on v2

--- a/solution.py
+++ b/solution.py
@@ -94,7 +94,7 @@
                 normed_ref[l, slot] = normed
         acc[...] = jnp.zeros_like(acc)
 
-        @pl.loop(0, tiles)
+        @pl.loop(0, tiles, unroll=True)
         def _(f):
             cols = columns(f)
             preact = dot(operand[...], up[l, :, cols])
@@ -120,7 +120,7 @@
             outg_ref[l, slot] = out_grad
         acc[...] = jnp.zeros_like(acc)
 
-        @pl.loop(0, tiles)
+        @pl.loop(0, tiles, unroll=True)
         def _(f):
             cols = columns(f)
             pre = (dot_t(operand[...], down[l, cols, :]) * slope[l, slot, :, cols]).astype(BF16)
@@ -258,17 +258,22 @@
     rates[me] = rate_ref[...]
     guess = guess_ref[...]
     state = guess
-    for copies in loads:
-        for copy in copies:
-            copy.wait()
     staged[...] = jnp.zeros_like(staged)
 
     @pl.when(me < n - 1)
     def _():
         state = guess
         for l in range(layers):
+            for copy in loads[l]:
+                copy.wait()
             state = forward(l, state, None, True)
         staged[...] = state
+
+    @pl.when(me == n - 1)
+    def _():
+        for copies in loads:
+            for copy in copies:
+                copy.wait()
 
     pl.semaphore_wait(barrier, n - 1 + group - 1)
 
@@ -401,7 +406,7 @@
 def gradients(normed, pre, hidden, outg, point, adjoint):
     layers, tokens, wcols = normed.shape
     fcols, ff, width = hidden.shape[2], pre.shape[2], outg.shape[2]
-    cuts = 4 if fcols % 512 == 0 and ff % 512 == 0 else 1
+    cuts = 1 if fcols % 512 == 0 and ff % 512 == 0 else 1
     rows = point.shape[0] // (layers * cuts)
     by_layer = lambda l, f: (l, 0, 0)
     by_cut = lambda l, f: (l, 0, f)

time: 60.8 us -> 51.6 us (0.85)
  Pallas kernels: 59.8 us -> 50.8 us
    pallas_call x1, Pallas kernels: 51.4 us -> 45.3 us  [relax(): pl.pallas_call(functools.partial(kernel, n, group, tile, sliced), out_sha...]
    pallas_call x1, Pallas kernels: 8.37 us -> 5.47 us  [gradients(): pl.pallas_call(gradients_kernel, grid=(layers, cuts), out_shape=(jax.Shap...]
where the time goes in v3:
time: 51.6 us; the launch traced here: 51.4 us
  Pallas kernels  50.8 us (98%)
  between operations  0.64 us (1%)
    pallas_call x1, Pallas kernels, relax(): pl.pallas_call(functools.partial(kernel, n, group, tile, sliced), out_sha...  45.3 us
    pallas_call x1, Pallas kernels, gradients(): pl.pallas_call(gradients_kernel, grid=(layers, cuts), out_shape=(jax.Shap...  5.47 us

profile of v3, /device:TPU:0, one launch (start us, length us, event | category | flops | bytes accessed | tf_op | source)
XLA Modules:
  0.0 51.4 jit_solution(12104431913638236683)
XLA Ops:
  0.6 45.3 %shard_map.93 = (f32[128,512]{1,0:T(8,128)}, f32[128,512]{1,0:T(8,128)}, bf16[2,2,128,256]{3,2,1,0:T(8,128)(2,1)}, bf16[2,2,128,2048]{3,2,1,0:T(8,128)(2,1)}, bf...) custom-call(f32[128,512]{1,0:T(8,128)} %bitcast.11, f32[128,512]{1,0:T(8,128)} %bitcast.12, ...), custom_call_target="tpu_custom_call" | custom-call | tf_op jit(solution)/shard_map/pallas_call | solution.py:348
  45.9 5.5 %shard_map.94 = (f32[2,256,2048]{2,1,0:T(8,128)}, f32[2,1024,512]{2,1,0:T(8,128)}, f32[128,512]{1,0:T(8,128)}, f32[128,512]{1,0:T(8,128)}) custom-call(bf16[2,256,256]{2,1,0:T(8,128)(2,1)} %bitcast.13, bf16[2,256,2048]{2,1,0:T(8,128)(2,1)} %bitcast.8, bf16[2,256,1024]{2,1,0:T(8,128)(2,1)} %bitcast.9, bf16[2,256,512]{2,1,0:T(8,128)(2,1)} %bitcast.10, ...), custom_call_target="tpu_custom_call" | custom-call | tf_op jit(solution)/shard_map/pallas_call | solution.py:414

commit v4 on v3

--- a/solution.py
+++ b/solution.py
@@ -336,7 +336,7 @@
     n, group = lax.axis_size("layer"), lax.axis_size("dp")
     tokens, width = c_guess.shape
     layers, _, ff = ups.shape
-    tile = min(ff, 512)
+    tile = min(ff, 1024)
     share = tokens // n
     sliced = (width // group) % 128 == 0 and (ff // group) % tile == 0
     wcols = width // group if sliced else width

time: 51.6 us -> 49.9 us (0.967)
  Pallas kernels: 50.8 us -> 49.1 us
    pallas_call x1, Pallas kernels: 45.3 us -> 43.6 us  [relax(): pl.pallas_call(functools.partial(kernel, n, group, tile, sliced), out_sha...]
where the time goes in v4:
time: 49.9 us; the launch traced here: 49.7 us
  Pallas kernels  49.1 us (98%)
  between operations  0.64 us (1%)
    pallas_call x1, Pallas kernels, relax(): pl.pallas_call(functools.partial(kernel, n, group, tile, sliced), out_sha...  43.6 us
    pallas_call x1, Pallas kernels, gradients(): pl.pallas_call(gradients_kernel, grid=(layers, cuts), out_shape=(jax.Shap...  5.47 us

profile of v4, /device:TPU:0, one launch (start us, length us, event | category | flops | bytes accessed | tf_op | source)
XLA Modules:
  0.0 49.7 jit_solution(10245888180706603904)
XLA Ops:
  0.6 43.6 %shard_map.93 = (f32[128,512]{1,0:T(8,128)}, f32[128,512]{1,0:T(8,128)}, bf16[2,2,128,256]{3,2,1,0:T(8,128)(2,1)}, bf16[2,2,128,2048]{3,2,1,0:T(8,128)(2,1)}, bf...) custom-call(f32[128,512]{1,0:T(8,128)} %bitcast.11, f32[128,512]{1,0:T(8,128)} %bitcast.12, ...), custom_call_target="tpu_custom_call" | custom-call | tf_op jit(solution)/shard_map/pallas_call | solution.py:348
  44.2 5.5 %shard_map.94 = (f32[2,256,2048]{2,1,0:T(8,128)}, f32[2,1024,512]{2,1,0:T(8,128)}, f32[128,512]{1,0:T(8,128)}, f32[128,512]{1,0:T(8,128)}) custom-call(bf16[2,256,256]{2,1,0:T(8,128)(2,1)} %bitcast.13, bf16[2,256,2048]{2,1,0:T(8,128)(2,1)} %bitcast.8, bf16[2,256,1024]{2,1,0:T(8,128)(2,1)} %bitcast.9, bf16[2,256,512]{2,1,0:T(8,128)(2,1)} %bitcast.10, ...), custom_call_target="tpu_custom_call" | custom-call | tf_op jit(solution)/shard_map/pallas_call | solution.py:414
